TPU v7x, 256 devices: a whole 4x4x8 slice. The times are simulated.
256 devices in a mesh: view: 2 (over core), sky: 128 (over z, x, y).
Axes of the slice: x: 4, y: 4, z: 8, core: 2. Of those that a mesh axis runs over, the one named last changes fastest.
Arguments:
- pixels: bfloat16 [2, 262144, 128], P('view', 'sky'), may hold values from -6 to 6
- cotangent: bfloat16 [2, 262144, 128], P('view', 'sky'), may hold values from -6 to 6
- filters: bfloat16 [4, 128, 128], replicated, may hold values from -0.25 to 0.25
- lap_tiles: bfloat16 [128, 24, 256, 256], P('sky'), may hold values from -0.15625 to 0.15625
- tile_target: int32 [128, 24], P('sky'), may hold values from 0 to 7
- tile_source: int32 [128, 24], P('sky'), may hold values from 0 to 15
- tile_count: int32 [128], P('sky'), may hold values from 12 to 24, as said below
- send_blocks: int32 [128, 4, 2], P('sky'), may hold values from 0 to 7
Outputs:
- outputs: bfloat16 [2, 262144, 128], P('view', 'sky')
- pixel_grad: bfloat16 [2, 262144, 128], P('view', 'sky')
- filter_grad: float32 [4, 128, 128], replicated
Inputs may be any that keep to these rules, and one draw needn't show every extreme that they name: `tile_count`: every device has at least half of 24 live tiles, and some device has exactly 24. `tile_source`: indices below 8 are own blocks, the others received ones.
All inputs are finite; a program needn't handle non-finite values.
Results may differ from a plain program's by a relative error of at most 0.017.
Values may be sent and summed in bfloat16 or wider, within the bound.
No kernel may reach another device: no remote copies, remote signals or barrier semaphores. Data moves between devices by JAX's collectives and lax.ppermute only.
A program may use at most 64 MiB of HBM per device.

v0:
```python
import math
import jax
import jax.numpy as jnp
from jax import lax
from jax.sharding import PartitionSpec as P

OFFSETS = (1, -1, 2, -2)


def passed_along(array, axis, by):
    size = lax.axis_size(axis)
    pairs = [(i, i + by) for i in range(size) if 0 <= i + by < size]
    return lax.ppermute(array, axis, pairs)


def spread_forward(pieces):
    return [passed_along(portion, "sky", offset) for offset, portion in zip(OFFSETS, pieces)]


def spread_backward(pieces):
    return [passed_along(portion, "sky", -offset) for offset, portion in zip(OFFSETS, pieces)]


def tile_products(values, tile_set, target, source, live_count, out_count, transposed):
    contraction = "tpq,tpc->tqc" if transposed else "tpq,tqc->tpc"
    picked = values[target] if transposed else values[source]
    routed = source if transposed else target
    products = jnp.einsum(contraction, tile_set, picked, preferred_element_type=jnp.float32)
    live_mask = jnp.arange(routed.shape[0]) < live_count
    routing = ((routed[None, :] == jnp.arange(out_count)[:, None]) & live_mask[None, :]).astype(
        jnp.float32
    )
    return jnp.einsum("bt,tpc->bpc", routing, products)


def per_device(
    pixels, cotangent, filters, lap_tiles, tile_target, tile_source, tile_count, send_blocks
):
    block_size = lap_tiles.shape[2]
    channels = pixels.shape[2]
    row_count = pixels.shape[1]
    block_count = row_count // block_size
    send_count = send_blocks.shape[2]
    ext_count = block_count + 4 * send_count
    tile_set = lap_tiles[0]
    target = tile_target[0]
    source = tile_source[0]
    live_count = tile_count[0]
    chosen = send_blocks[0]

    def forward_pieces(blocks):
        return [blocks[chosen[number]] for number in range(4)]

    def forward_finish(blocks, arrived):
        extended = jnp.concatenate([blocks] + arrived, axis=0)
        return tile_products(extended, tile_set, target, source, live_count, block_count, False)

    def transposed_start(blocks):
        slot_sums = tile_products(blocks, tile_set, target, source, live_count, ext_count, True)
        pieces = [
            slot_sums[block_count + number * send_count : block_count + (number + 1) * send_count]
            for number in range(4)
        ]
        return (slot_sums, pieces)

    def transposed_finish(slot_sums, arrived):
        combined = slot_sums[:block_count]
        for number in range(4):
            routing = (chosen[number][None, :] == jnp.arange(block_count)[:, None]).astype(
                jnp.float32
            )
            combined = combined + jnp.einsum("bj,jqc->bqc", routing, arrived[number])
        return combined

    def apply_forward(blocks):
        return forward_finish(blocks, spread_forward(forward_pieces(blocks)))

    def apply_transposed(blocks):
        slot_sums, pieces = transposed_start(blocks)
        return transposed_finish(slot_sums, spread_backward(pieces))

    upstream = cotangent[0]

    def filter_term(member):
        return jnp.einsum("pc,pd->cd", member, upstream, preferred_element_type=jnp.float32)

    base = pixels[0].reshape(block_count, block_size, channels)
    pulled = [
        jnp.einsum(
            "pd,cd->pc", upstream, filters[order], preferred_element_type=jnp.float32
        ).reshape(block_count, block_size, channels)
        for order in range(4)
    ]
    adj_three = pulled[3]
    grad_terms = [filter_term(pixels[0])]
    cheb_one = apply_forward(base).astype(jnp.bfloat16)
    grad_terms.append(filter_term(cheb_one.reshape(row_count, channels)))
    cheb_two = (2.0 * apply_forward(cheb_one) - base.astype(jnp.float32)).astype(jnp.bfloat16)
    grad_terms.append(filter_term(cheb_two.reshape(row_count, channels)))
    cheb_three = (2.0 * apply_forward(cheb_two) - cheb_one.astype(jnp.float32)).astype(jnp.bfloat16)
    grad_terms.append(filter_term(cheb_three.reshape(row_count, channels)))
    adj_two = pulled[2] + 2.0 * apply_transposed(adj_three.astype(jnp.bfloat16))
    adj_one = pulled[1] + 2.0 * apply_transposed(adj_two.astype(jnp.bfloat16)) - adj_three
    adj_zero = pulled[0] + apply_transposed(adj_one.astype(jnp.bfloat16)) - adj_two
    flattened = [
        member.reshape(row_count, channels) for member in (base, cheb_one, cheb_two, cheb_three)
    ]
    result = jnp.dot(flattened[0], filters[0], preferred_element_type=jnp.float32)
    for order in range(1, 4):
        result = result + jnp.dot(
            flattened[order], filters[order], preferred_element_type=jnp.float32
        )
    outputs = result.astype(jnp.bfloat16).reshape(1, row_count, channels)
    pixel_grad = adj_zero.astype(jnp.bfloat16).reshape(1, row_count, channels)
    stacked = lax.psum(jnp.stack(grad_terms), ("view", "sky"))
    scale = 1.0 / math.sqrt(lax.axis_size("view") * lax.axis_size("sky") * row_count)
    return (outputs, pixel_grad, stacked * scale)


def solution(mesh):
    return jax.shard_map(
        per_device,
        mesh=mesh,
        in_specs=(
            P("view", "sky", None),
            P("view", "sky", None),
            P(),
            P("sky", None, None, None),
            P("sky", None),
            P("sky", None),
            P("sky"),
            P("sky", None, None),
        ),
        out_specs=(P("view", "sky", None), P("view", "sky", None), P()),
        check_vma=False,
    )
```

profile of v0, /device:TPU:2, one launch (start us, length us, event | category | flops | bytes accessed | tf_op | source)
XLA Modules:
  0.0 553.1 jit_solution(11454189926382703795)
XLA Ops:
  10.6 3.0 gather_fusion.15
  13.6 3.3 fusion.16
  16.9 2.8 copy.48
  24.6 5.1 collective-permute-start.15
  29.7 3.2 collective-permute-start.14
  32.9 3.5 collective-permute-start.13
  44.8 5.5 collective-permute-start.1
  67.9 6.3 %collective-permute-start.3 = (bf16[2,256,128]{2,1,0:T(8,128)(2,1)}, bf16[2,256,128]{2,1,0:T(8,128)(2,1)S(1)}, u32[]{:S(2)}, u32[]{:S(2)}) collective-permute-start(bf16[2,256,128]{2,1,0:T(8,128)(2,1)} %gather_fusion.3), channel_id=1, source_target_pairs={{2,0},{3,1},{4,2},{5,3},{6,4},{7,5},{8,6},{9,7},{10,8},{11,9},{12,... | collective-permute-start | bytes 393224 | tf_op jit(solution)/shard_map/ppermute | solution.py:13
  78.8 3.3 gather_fusion.4
  82.1 3.8 fusion.22
  85.8 2.8 copy.42
  107.8 3.1 gather_fusion.16
  111.0 3.2 fusion.14
  119.9 6.8 %collective-permute-start.19 = (bf16[2,256,128]{2,0,1:T(2,128)(2,1)}, bf16[2,256,128]{2,0,1:T(2,128)(2,1)}, u32[]{:S(2)}, u32[]{:S(2)}) collective-permute-start(bf16[2,256,128]{2,0,1:T(2,128)(2,1)} %get-tuple-element.12), channel_id=1, source_target_pairs={{0,2},{1,3},{2,4},{3,5},{4,6},{5,7},{6,8},{7,9},{8,10},{9,11},{10,... | collective-permute-start | bytes 393224 | tf_op jit(solution)/shard_map/ppermute | solution.py:13
  129.0 6.3 %collective-permute-start.5 = (bf16[2,256,128]{2,0,1:T(2,128)(2,1)S(1)}, bf16[2,256,128]{2,0,1:T(2,128)(2,1)}, u32[]{:S(2)}, u32[]{:S(2)}) collective-permute-start(bf16[2,256,128]{2,0,1:T(2,128)(2,1)S(1)} %copy.18), channel_id=1, source_target_pairs={{1,0},{2,1},{3,2},{4,3},{5,4},{6,5},{7,6},{8,7},{9,8},{10,9},{11,1... | collective-permute-start | bytes 393224 | tf_op jit(solution)/shard_map/ppermute | solution.py:13
  137.6 6.3 %collective-permute-start.7 = (bf16[2,256,128]{2,0,1:T(2,128)(2,1)S(1)}, bf16[2,256,128]{2,0,1:T(2,128)(2,1)S(1)}, u32[]{:S(2)}, u32[]{:S(2)}) collective-permute-start(bf16[2,256,128]{2,0,1:T(2,128)(2,1)S(1)} %copy.22), channel_id=1, source_target_pairs={{2,0},{3,1},{4,2},{5,3},{6,4},{7,5},{8,6},{9,7},{10,8},{11,9},{12,... | collective-permute-start | bytes 393224 | tf_op jit(solution)/shard_map/ppermute | solution.py:13
  150.1 6.0 %collective-permute-start.16 = (bf16[2,256,128]{2,0,1:T(2,128)(2,1)}, bf16[2,256,128]{2,0,1:T(2,128)(2,1)}, u32[]{:S(2)}, u32[]{:S(2)}) collective-permute-start(bf16[2,256,128]{2,0,1:T(2,128)(2,1)} %get-tuple-element.11), channel_id=1, source_target_pairs={{1,0},{2,1},{3,2},{4,3},{5,4},{6,5},{7,6},{8,7},{9,8},{10,9},{11,1... | collective-permute-start | bytes 393224 | tf_op jit(solution)/shard_map/ppermute | solution.py:13
  156.1 6.4 %concatenate.10 = bf16[16,256,128]{2,0,1:T(8,128)(2,1)} concatenate(bf16[8,256,128]{2,0,1:T(8,128)(2,1)} %copy-done.6, bf16[2,256,128]{2,0,1:T(2,128)(2,1)} %collective-permute-done.4, bf16[2,256,128]{2,0,1:T(2,128)(2,1)} %collective-permute-done.5, bf16[2,256,128]{2,0,1:T(2,128)(2,1)S(1)} %collective-permute-done.6, bf16[2,256,128]{2,0,1:T(2,128)(2,1)S(1)} %collective-permute-done.7), dimensions={0} | concatenate | bytes 2097152 | tf_op jit(solution)/shard_map/concatenate | solution.py:55
  165.0 3.3 gather_fusion.9
  168.3 3.8 fusion.20
  194.5 3.1 gather_fusion.17
  197.6 3.2 fusion.12
  207.9 2.8 collective-permute-start.21
  210.7 4.6 collective-permute-start.23
  215.3 5.4 collective-permute-start.20
  220.8 3.3 collective-permute-start.10
  226.4 5.1 collective-permute-start.11
  234.2 6.3 %collective-permute-start.9 = (bf16[2,256,128]{2,0,1:T(2,128)(2,1)S(1)}, bf16[2,256,128]{2,0,1:T(2,128)(2,1)}, u32[]{:S(2)}, u32[]{:S(2)}) collective-permute-start(bf16[2,256,128]{2,0,1:T(2,128)(2,1)S(1)} %copy.29), channel_id=1, source_target_pairs={{1,0},{2,1},{3,2},{4,3},{5,4},{6,5},{7,6},{8,7},{9,8},{10,9},{11,1... | collective-permute-start | bytes 393224 | tf_op jit(solution)/shard_map/ppermute | solution.py:13
  242.8 6.5 %concatenate.11 = bf16[16,256,128]{2,0,1:T(8,128)(2,1)} concatenate(bf16[8,256,128]{2,0,1:T(8,128)(2,1)} %copy-done.13, bf16[2,256,128]{2,0,1:T(2,128)(2,1)} %collective-permute-done.8, bf16[2,256,128]{2,0,1:T(2,128)(2,1)} %collective-permute-done.9, bf16[2,256,128]{2,0,1:T(2,128)(2,1)} %collective-permute-done.10, bf16[2,256,128]{2,0,1:T(2,128)(2,1)S(1)} %collective-permute-done.11), dimensions={0} | concatenate | bytes 2097152 | tf_op jit(solution)/shard_map/concatenate | solution.py:55
  251.7 3.3 gather_fusion.14
  255.0 3.7 fusion.18
  267.6 277.0 %all-reduce.2.cloned.1.call-done = f32[4,128,128]{2,1,0:T(8,128)} async-done(((f32[4,128,128]{2,1,0:T(8,128)}), f32[4,128,128]{2,1,0:T(8,128)}) %all-reduce.2.cloned.1.call-update) | async-done | bytes 262160 | tf_op jit(solution)/shard_map/psum | solution.py:115
  (197 shorter events, 125.6 us)
Async XLA Ops:
  7.2 537.4 %all-reduce.2.cloned.1.call-start = ((), (), s32[]{:S(2)}) async-start(), calls=%async_computation | async-start | bytes 524288 | tf_op jit(solution)/shard_map/psum | solution.py:115
  23.5 26.8 %copy-start.21 = (bf16[4,128,128]{2,1,0:T(8,128)(2,1)S(1)}, bf16[4,128,128]{2,1,0:T(8,128)(2,1)}, u32[]{:S(2)}) copy-start(bf16[4,128,128]{2,1,0:T(8,128)(2,1)} %param.10) | copy-start | bytes 393220
  24.6 75.7 %collective-permute-start.15 = (bf16[2,256,128]{2,0,1:T(2,128)(2,1)}, bf16[2,256,128]{2,0,1:T(2,128)(2,1)}, u32[]{:S(2)}, u32[]{:S(2)}) collective-permute-start(bf16[2,256,128]{2,0,1:T(2,128)(2,1)} %get-tuple-element.16), channel_id=1, source_target_pairs={{0,2},{1,3},{2,4},{3,5},{4,6},{5,7},{6,8},{7,9},{8,10},{9,11},{10,... | collective-permute-start | bytes 393224 | tf_op jit(solution)/shard_map/ppermute | solution.py:13
  29.7 72.1 %collective-permute-start.14 = (bf16[2,256,128]{2,0,1:T(2,128)(2,1)}, bf16[2,256,128]{2,0,1:T(2,128)(2,1)}, u32[]{:S(2)}, u32[]{:S(2)}) collective-permute-start(bf16[2,256,128]{2,0,1:T(2,128)(2,1)} %get-tuple-element.17), channel_id=1, source_target_pairs={{2,0},{3,1},{4,2},{5,3},{6,4},{7,5},{8,6},{9,7},{10,8},{11,9},{12,... | collective-permute-start | bytes 393224 | tf_op jit(solution)/shard_map/ppermute | solution.py:13
  32.9 70.3 %collective-permute-start.13 = (bf16[2,256,128]{2,0,1:T(2,128)(2,1)}, bf16[2,256,128]{2,0,1:T(2,128)(2,1)}, u32[]{:S(2)}, u32[]{:S(2)}) collective-permute-start(bf16[2,256,128]{2,0,1:T(2,128)(2,1)} %get-tuple-element.18), channel_id=1, source_target_pairs={{0,1},{1,2},{2,3},{3,4},{4,5},{5,6},{6,7},{7,8},{8,9},{9,10},{10,1... | collective-permute-start | bytes 393224 | tf_op jit(solution)/shard_map/ppermute | solution.py:13
  39.4 25.9 %collective-permute-start = (bf16[2,256,128]{2,1,0:T(8,128)(2,1)}, bf16[2,256,128]{2,1,0:T(8,128)(2,1)S(1)}, u32[]{:S(2)}, u32[]{:S(2)}) collective-permute-start(bf16[2,256,128]{2,1,0:T(8,128)(2,1)} %gather_fusion), channel_id=1, source_target_pairs={{0,1},{1,2},{2,3},{3,4},{4,5},{5,6},{6,7},{7,8},{8,9},{9,10},{10,1... | collective-permute-start | bytes 393224 | tf_op jit(solution)/shard_map/ppermute | solution.py:13
  44.8 23.0 %collective-permute-start.1 = (bf16[2,256,128]{2,1,0:T(8,128)(2,1)}, bf16[2,256,128]{2,1,0:T(8,128)(2,1)S(1)}, u32[]{:S(2)}, u32[]{:S(2)}) collective-permute-start(bf16[2,256,128]{2,1,0:T(8,128)(2,1)} %gather_fusion.1), channel_id=1, source_target_pairs={{1,0},{2,1},{3,2},{4,3},{5,4},{6,5},{7,6},{8,7},{9,8},{10,9},{11,1... | collective-permute-start | bytes 393224 | tf_op jit(solution)/shard_map/ppermute | solution.py:13
  65.3 9.6 %collective-permute-start.2 = (bf16[2,256,128]{2,1,0:T(8,128)(2,1)}, bf16[2,256,128]{2,1,0:T(8,128)(2,1)S(1)}, u32[]{:S(2)}, u32[]{:S(2)}) collective-permute-start(bf16[2,256,128]{2,1,0:T(8,128)(2,1)} %gather_fusion.2), channel_id=1, source_target_pairs={{0,2},{1,3},{2,4},{3,5},{4,6},{5,7},{6,8},{7,9},{8,10},{9,11},{10,... | collective-permute-start | bytes 393224 | tf_op jit(solution)/shard_map/ppermute | solution.py:13
  67.9 10.3 %collective-permute-start.3 = (bf16[2,256,128]{2,1,0:T(8,128)(2,1)}, bf16[2,256,128]{2,1,0:T(8,128)(2,1)S(1)}, u32[]{:S(2)}, u32[]{:S(2)}) collective-permute-start(bf16[2,256,128]{2,1,0:T(8,128)(2,1)} %gather_fusion.3), channel_id=1, source_target_pairs={{2,0},{3,1},{4,2},{5,3},{6,4},{7,5},{8,6},{9,7},{10,8},{11,9},{12,... | collective-permute-start | bytes 393224 | tf_op jit(solution)/shard_map/ppermute | solution.py:13
  74.8 29.6 %collective-permute-start.12 = (bf16[2,256,128]{2,0,1:T(2,128)(2,1)}, bf16[2,256,128]{2,0,1:T(2,128)(2,1)}, u32[]{:S(2)}, u32[]{:S(2)}) collective-permute-start(bf16[2,256,128]{2,0,1:T(2,128)(2,1)} %get-tuple-element.15), channel_id=1, source_target_pairs={{1,0},{2,1},{3,2},{4,3},{5,4},{6,5},{7,6},{8,7},{9,8},{10,9},{11,1... | collective-permute-start | bytes 393224 | tf_op jit(solution)/shard_map/ppermute | solution.py:13
  118.8 26.4 %copy-start.11 = (f32[16,256,128]{2,0,1:T(8,128)}, f32[16,256,128]{2,0,1:T(8,128)S(1)}, u32[]{:S(2)}) copy-start(f32[16,256,128]{2,0,1:T(8,128)S(1)} %fusion.2) | copy-start | bytes 6291460
  118.8 25.1 %copy-start.8 = (bf16[8,256,128]{2,1,0:T(8,128)(2,1)S(1)}, bf16[8,256,128]{2,1,0:T(8,128)(2,1)}, u32[]{:S(2)}) copy-start(bf16[8,256,128]{2,1,0:T(8,128)(2,1)} %copy.14) | copy-start | bytes 1572868
  118.8 25.1 %copy-start.17 = (f32[2048,128]{1,0:T(8,128)S(1)}, f32[2048,128]{1,0:T(8,128)}, u32[]{:S(2)}) copy-start(f32[2048,128]{1,0:T(8,128)} %fusion.70) | copy-start | bytes 3145732
  119.9 67.0 %collective-permute-start.19 = (bf16[2,256,128]{2,0,1:T(2,128)(2,1)}, bf16[2,256,128]{2,0,1:T(2,128)(2,1)}, u32[]{:S(2)}, u32[]{:S(2)}) collective-permute-start(bf16[2,256,128]{2,0,1:T(2,128)(2,1)} %get-tuple-element.12), channel_id=1, source_target_pairs={{0,2},{1,3},{2,4},{3,5},{4,6},{5,7},{6,8},{7,9},{8,10},{9,11},{10,... | collective-permute-start | bytes 393224 | tf_op jit(solution)/shard_map/ppermute | solution.py:13
  126.9 19.2 %collective-permute-start.4 = (bf16[2,256,128]{2,0,1:T(2,128)(2,1)S(1)}, bf16[2,256,128]{2,0,1:T(2,128)(2,1)}, u32[]{:S(2)}, u32[]{:S(2)}) collective-permute-start(bf16[2,256,128]{2,0,1:T(2,128)(2,1)S(1)} %copy.16), channel_id=1, source_target_pairs={{0,1},{1,2},{2,3},{3,4},{4,5},{5,6},{6,7},{7,8},{8,9},{9,10},{10,1... | collective-permute-start | bytes 393224 | tf_op jit(solution)/shard_map/ppermute | solution.py:13
  129.0 19.1 %collective-permute-start.5 = (bf16[2,256,128]{2,0,1:T(2,128)(2,1)S(1)}, bf16[2,256,128]{2,0,1:T(2,128)(2,1)}, u32[]{:S(2)}, u32[]{:S(2)}) collective-permute-start(bf16[2,256,128]{2,0,1:T(2,128)(2,1)S(1)} %copy.18), channel_id=1, source_target_pairs={{1,0},{2,1},{3,2},{4,3},{5,4},{6,5},{7,6},{8,7},{9,8},{10,9},{11,1... | collective-permute-start | bytes 393224 | tf_op jit(solution)/shard_map/ppermute | solution.py:13
  135.5 14.5 %collective-permute-start.6 = (bf16[2,256,128]{2,0,1:T(2,128)(2,1)S(1)}, bf16[2,256,128]{2,0,1:T(2,128)(2,1)S(1)}, u32[]{:S(2)}, u32[]{:S(2)}) collective-permute-start(bf16[2,256,128]{2,0,1:T(2,128)(2,1)S(1)} %copy.20), channel_id=1, source_target_pairs={{0,2},{1,3},{2,4},{3,5},{4,6},{5,7},{6,8},{7,9},{8,10},{9,11},{10,... | collective-permute-start | bytes 393224 | tf_op jit(solution)/shard_map/ppermute | solution.py:13
  137.6 18.5 %collective-permute-start.7 = (bf16[2,256,128]{2,0,1:T(2,128)(2,1)S(1)}, bf16[2,256,128]{2,0,1:T(2,128)(2,1)S(1)}, u32[]{:S(2)}, u32[]{:S(2)}) collective-permute-start(bf16[2,256,128]{2,0,1:T(2,128)(2,1)S(1)} %copy.22), channel_id=1, source_target_pairs={{2,0},{3,1},{4,2},{5,3},{6,4},{7,5},{8,6},{9,7},{10,8},{11,9},{12,... | collective-permute-start | bytes 393224 | tf_op jit(solution)/shard_map/ppermute | solution.py:13
  146.2 42.2 %collective-permute-start.18 = (bf16[2,256,128]{2,0,1:T(2,128)(2,1)}, bf16[2,256,128]{2,0,1:T(2,128)(2,1)}, u32[]{:S(2)}, u32[]{:S(2)}) collective-permute-start(bf16[2,256,128]{2,0,1:T(2,128)(2,1)} %get-tuple-element.13), channel_id=1, source_target_pairs={{2,0},{3,1},{4,2},{5,3},{6,4},{7,5},{8,6},{9,7},{10,8},{11,9},{12,... | collective-permute-start | bytes 393224 | tf_op jit(solution)/shard_map/ppermute | solution.py:13
  148.1 41.6 %collective-permute-start.17 = (bf16[2,256,128]{2,0,1:T(2,128)(2,1)}, bf16[2,256,128]{2,0,1:T(2,128)(2,1)}, u32[]{:S(2)}, u32[]{:S(2)}) collective-permute-start(bf16[2,256,128]{2,0,1:T(2,128)(2,1)} %get-tuple-element.14), channel_id=1, source_target_pairs={{0,1},{1,2},{2,3},{3,4},{4,5},{5,6},{6,7},{7,8},{8,9},{9,10},{10,1... | collective-permute-start | bytes 393224 | tf_op jit(solution)/shard_map/ppermute | solution.py:13
  150.1 41.0 %collective-permute-start.16 = (bf16[2,256,128]{2,0,1:T(2,128)(2,1)}, bf16[2,256,128]{2,0,1:T(2,128)(2,1)}, u32[]{:S(2)}, u32[]{:S(2)}) collective-permute-start(bf16[2,256,128]{2,0,1:T(2,128)(2,1)} %get-tuple-element.11), channel_id=1, source_target_pairs={{1,0},{2,1},{3,2},{4,3},{5,4},{6,5},{7,6},{8,7},{9,8},{10,9},{11,1... | collective-permute-start | bytes 393224 | tf_op jit(solution)/shard_map/ppermute | solution.py:13
  205.4 19.0 %copy-start.22 = (bf16[2,256,128]{2,1,0:T(8,128)(2,1)S(1)}, bf16[2,256,128]{2,1,0:T(8,128)(2,1)}, u32[]{:S(2)}) copy-start(bf16[2,256,128]{2,1,0:T(8,128)(2,1)} %gather_fusion.11) | copy-start | bytes 393220
  205.5 19.2 %copy-start.7 = (bf16[8,256,128]{2,1,0:T(8,128)(2,1)S(1)}, bf16[8,256,128]{2,1,0:T(8,128)(2,1)}, u32[]{:S(2)}) copy-start(bf16[8,256,128]{2,1,0:T(8,128)(2,1)} %copy.25) | copy-start | bytes 1572868
  205.5 19.2 %copy-start.20 = (f32[2048,128]{1,0:T(8,128)S(1)}, f32[2048,128]{1,0:T(8,128)}, u32[]{:S(2)}) copy-start(f32[2048,128]{1,0:T(8,128)} %convolution_add_fusion.2) | copy-start | bytes 3145732
  205.8 20.5 %collective-permute-start.22 = (bf16[2,256,128]{2,0,1:T(2,128)(2,1)S(1)}, bf16[2,256,128]{2,0,1:T(2,128)(2,1)S(1)}, u32[]{:S(2)}, u32[]{:S(2)}) collective-permute-start(bf16[2,256,128]{2,0,1:T(2,128)(2,1)S(1)} %get-tuple-element.9), channel_id=1, source_target_pairs={{2,0},{3,1},{4,2},{5,3},{6,4},{7,5},{8,6},{9,7},{10,8},{11,9},{12,... | collective-permute-start | bytes 393224 | tf_op jit(solution)/shard_map/ppermute | solution.py:13
  207.9 24.0 %collective-permute-start.21 = (bf16[2,256,128]{2,0,1:T(2,128)(2,1)S(1)}, bf16[2,256,128]{2,0,1:T(2,128)(2,1)S(1)}, u32[]{:S(2)}, u32[]{:S(2)}) collective-permute-start(bf16[2,256,128]{2,0,1:T(2,128)(2,1)S(1)} %get-tuple-element.10), channel_id=1, source_target_pairs={{0,1},{1,2},{2,3},{3,4},{4,5},{5,6},{6,7},{7,8},{8,9},{9,10},{10,1... | collective-permute-start | bytes 393224 | tf_op jit(solution)/shard_map/ppermute | solution.py:13
  210.7 23.5 %collective-permute-start.23 = (bf16[2,256,128]{2,0,1:T(2,128)(2,1)S(1)}, bf16[2,256,128]{2,0,1:T(2,128)(2,1)S(1)}, u32[]{:S(2)}, u32[]{:S(2)}) collective-permute-start(bf16[2,256,128]{2,0,1:T(2,128)(2,1)S(1)} %get-tuple-element.8), channel_id=1, source_target_pairs={{0,2},{1,3},{2,4},{3,5},{4,6},{5,7},{6,8},{7,9},{8,10},{9,11},{10,... | collective-permute-start | bytes 393224 | tf_op jit(solution)/shard_map/ppermute | solution.py:13
  215.3 25.6 %collective-permute-start.20 = (bf16[2,256,128]{2,0,1:T(2,128)(2,1)S(1)}, bf16[2,256,128]{2,0,1:T(2,128)(2,1)S(1)}, u32[]{:S(2)}, u32[]{:S(2)}) collective-permute-start(bf16[2,256,128]{2,0,1:T(2,128)(2,1)S(1)} %get-tuple-element.7), channel_id=1, source_target_pairs={{1,0},{2,1},{3,2},{4,3},{5,4},{6,5},{7,6},{8,7},{9,8},{10,9},{11,1... | collective-permute-start | bytes 393224 | tf_op jit(solution)/shard_map/ppermute | solution.py:13
  220.8 21.7 %collective-permute-start.10 = (bf16[2,256,128]{2,0,1:T(2,128)(2,1)S(1)}, bf16[2,256,128]{2,0,1:T(2,128)(2,1)}, u32[]{:S(2)}, u32[]{:S(2)}) collective-permute-start(bf16[2,256,128]{2,0,1:T(2,128)(2,1)S(1)} %copy.31), channel_id=1, source_target_pairs={{0,2},{1,3},{2,4},{3,5},{4,6},{5,7},{6,8},{7,9},{8,10},{9,11},{10,... | collective-permute-start | bytes 393224 | tf_op jit(solution)/shard_map/ppermute | solution.py:13
  226.4 16.2 %collective-permute-start.11 = (bf16[2,256,128]{2,0,1:T(2,128)(2,1)S(1)}, bf16[2,256,128]{2,0,1:T(2,128)(2,1)S(1)}, u32[]{:S(2)}, u32[]{:S(2)}) collective-permute-start(bf16[2,256,128]{2,0,1:T(2,128)(2,1)S(1)} %copy.33), channel_id=1, source_target_pairs={{2,0},{3,1},{4,2},{5,3},{6,4},{7,5},{8,6},{9,7},{10,8},{11,9},{12,... | collective-permute-start | bytes 393224 | tf_op jit(solution)/shard_map/ppermute | solution.py:13
  231.9 10.7 %collective-permute-start.8 = (bf16[2,256,128]{2,0,1:T(2,128)(2,1)S(1)}, bf16[2,256,128]{2,0,1:T(2,128)(2,1)}, u32[]{:S(2)}, u32[]{:S(2)}) collective-permute-start(bf16[2,256,128]{2,0,1:T(2,128)(2,1)S(1)} %copy.27), channel_id=1, source_target_pairs={{0,1},{1,2},{2,3},{3,4},{4,5},{5,6},{6,7},{7,8},{8,9},{9,10},{10,1... | collective-permute-start | bytes 393224 | tf_op jit(solution)/shard_map/ppermute | solution.py:13
  234.2 8.5 %collective-permute-start.9 = (bf16[2,256,128]{2,0,1:T(2,128)(2,1)S(1)}, bf16[2,256,128]{2,0,1:T(2,128)(2,1)}, u32[]{:S(2)}, u32[]{:S(2)}) collective-permute-start(bf16[2,256,128]{2,0,1:T(2,128)(2,1)S(1)} %copy.29), channel_id=1, source_target_pairs={{1,0},{2,1},{3,2},{4,3},{5,4},{6,5},{7,6},{8,7},{9,8},{10,9},{11,1... | collective-permute-start | bytes 393224 | tf_op jit(solution)/shard_map/ppermute | solution.py:13
  (32 other events, 177.5 us)
Sparse Core Ops, SparseCore 0:
  265.3 279.2 all-reduce.1
where the time goes:
time: 556 us; the launch traced here: 553 us
  waiting for transfers between devices  278 us (50%)
  local copies, waits for them, and re-layouts  95.7 us (17%)
  starting transfers between devices  94.5 us (17%)
  matrix products  64.3 us (12%)
  between operations  15.6 us (3%)
    psum x1, waiting for transfers between devices, per_device(): stacked = lax.psum(jnp.stack(grad_terms), ('view', 'sky'))  277 us
    ppermute x24, starting transfers between devices, passed_along(): return lax.ppermute(array, axis, pairs)  94.5 us
    gather x20, local copies, waits for them, and re-layouts, forward_pieces(): return [blocks[chosen[number]] for number in range(4)]  26.8 us
    dot_general x6, matrix products, tile_products(): jnp.einsum(contraction, tile_set, picked, preferred_element_type=jnp.floa...  20.9 us
    gather x6, local copies, waits for them, and re-layouts, tile_products(): picked = values[target] if transposed else values[source]  19.1 us
    concatenate x5, local copies, waits for them, and re-layouts, forward_finish(): extended = jnp.concatenate([blocks] + arrived, axis=0)  18.5 us
    dot_general x6, local copies, waits for them, and re-layouts, tile_products(): jnp.einsum(contraction, tile_set, picked, preferred_element_type=jnp.floa...  16.5 us
    dot_general x12, matrix products, transposed_finish(): combined = combined + jnp.einsum('bj,jqc->bqc', routing, arrived[number])  15 us
  transfers between devices with their start and end apart: 25, of which 3 were waited for; matrix products, arithmetic and copies ran while one was open for 17% of the time, Pallas kernels for 0%

commit v1 on v0

--- a/solution.py
+++ b/solution.py
@@ -112,7 +112,9 @@
         )
     outputs = result.astype(jnp.bfloat16).reshape(1, row_count, channels)
     pixel_grad = adj_zero.astype(jnp.bfloat16).reshape(1, row_count, channels)
-    stacked = lax.psum(jnp.stack(grad_terms), ("view", "sky"))
+    xin = jnp.stack(grad_terms)
+    big = lax.psum(xin, "view")
+    stacked = lax.psum(big, "sky")
     scale = 1.0 / math.sqrt(lax.axis_size("view") * lax.axis_size("sky") * row_count)
     return (outputs, pixel_grad, stacked * scale)
 

time: 556 us -> 546 us (0.982)
  waiting for transfers between devices: 278 us -> 261 us
  matrix products: 64.3 us -> 71.4 us
    psum x1 -> x2, waiting for transfers between devices: 277 us -> 261 us  [the longest x1 214 us: per_device(): stacked = lax.psum(big, 'sky')]
    dot_general x12, matrix products: 15 us -> 23.5 us  [transposed_finish(): combined = combined + jnp.einsum('bj,jqc->bqc', routing, arrived[number])]
  transfers between devices with their start and end apart: 25 -> 26, of which waited for: 3 -> 3; matrix products, arithmetic and copies ran while one was open for 17% -> 22% of each run, Pallas kernels for 0% -> 0%
where the time goes in v1:
time: 546 us; the launch traced here: 542 us
  waiting for transfers between devices  261 us (48%)
  local copies, waits for them, and re-layouts  97.2 us (18%)
  starting transfers between devices  91.7 us (17%)
  matrix products  71.4 us (13%)
  between operations  15.7 us (3%)
    psum x1, waiting for transfers between devices, per_device(): stacked = lax.psum(big, 'sky')  214 us
    ppermute x24, starting transfers between devices, passed_along(): return lax.ppermute(array, axis, pairs)  91.6 us
    psum x1, waiting for transfers between devices, per_device(): big = lax.psum(xin, 'view')  46.2 us
    gather x20, local copies, waits for them, and re-layouts, forward_pieces(): return [blocks[chosen[number]] for number in range(4)]  26.8 us
    dot_general x12, matrix products, transposed_finish(): combined = combined + jnp.einsum('bj,jqc->bqc', routing, arrived[number])  23.5 us
    dot_general x6, matrix products, tile_products(): jnp.einsum(contraction, tile_set, picked, preferred_element_type=jnp.floa...  21 us
    gather x6, local copies, waits for them, and re-layouts, tile_products(): picked = values[target] if transposed else values[source]  19.1 us
    concatenate x5, local copies, waits for them, and re-layouts, forward_finish(): extended = jnp.concatenate([blocks] + arrived, axis=0)  18.7 us
  transfers between devices with their start and end apart: 26, of which 3 were waited for; matrix products, arithmetic and copies ran while one was open for 22% of the time, Pallas kernels for 0%

profile of v1, /device:TPU:2, one launch (start us, length us, event | category | flops | bytes accessed | tf_op | source)
XLA Modules:
  0.0 542.4 jit_solution(11402797703340161463)
XLA Ops:
  10.6 3.0 gather_fusion.15
  13.6 3.3 fusion.16
  16.9 2.8 copy.48
  24.7 5.1 collective-permute-start.15
  29.8 3.2 collective-permute-start.14
  32.9 3.5 collective-permute-start.13
  44.8 5.5 %collective-permute-start.1 = (bf16[2,256,128]{2,1,0:T(8,128)(2,1)}, bf16[2,256,128]{2,1,0:T(8,128)(2,1)S(1)}, u32[]{:S(2)}, u32[]{:S(2)}) collective-permute-start(bf16[2,256,128]{2,1,0:T(8,128)(2,1)} %gather_fusion.1), channel_id=1, source_target_pairs={{1,0},{2,1},{3,2},{4,3},{5,4},{6,5},{7,6},{8,7},{9,8},{10,9},{11,1... | collective-permute-start | bytes 393224 | tf_op jit(solution)/shard_map/ppermute | solution.py:13
  67.9 6.3 %collective-permute-start.3 = (bf16[2,256,128]{2,1,0:T(8,128)(2,1)}, bf16[2,256,128]{2,1,0:T(8,128)(2,1)S(1)}, u32[]{:S(2)}, u32[]{:S(2)}) collective-permute-start(bf16[2,256,128]{2,1,0:T(8,128)(2,1)} %gather_fusion.3), channel_id=1, source_target_pairs={{2,0},{3,1},{4,2},{5,3},{6,4},{7,5},{8,6},{9,7},{10,8},{11,9},{12,... | collective-permute-start | bytes 393224 | tf_op jit(solution)/shard_map/ppermute | solution.py:13
  78.8 3.3 gather_fusion.4
  82.1 3.8 fusion.22
  108.0 3.1 gather_fusion.16
  111.1 3.2 fusion.14
  120.1 6.8 %collective-permute-start.19 = (bf16[2,256,128]{2,0,1:T(2,128)(2,1)}, bf16[2,256,128]{2,0,1:T(2,128)(2,1)}, u32[]{:S(2)}, u32[]{:S(2)}) collective-permute-start(bf16[2,256,128]{2,0,1:T(2,128)(2,1)} %get-tuple-element.12), channel_id=1, source_target_pairs={{0,2},{1,3},{2,4},{3,5},{4,6},{5,7},{6,8},{7,9},{8,10},{9,11},{10,... | collective-permute-start | bytes 393224 | tf_op jit(solution)/shard_map/ppermute | solution.py:13
  129.2 6.3 %collective-permute-start.5 = (bf16[2,256,128]{2,0,1:T(2,128)(2,1)S(1)}, bf16[2,256,128]{2,0,1:T(2,128)(2,1)}, u32[]{:S(2)}, u32[]{:S(2)}) collective-permute-start(bf16[2,256,128]{2,0,1:T(2,128)(2,1)S(1)} %copy.18), channel_id=1, source_target_pairs={{1,0},{2,1},{3,2},{4,3},{5,4},{6,5},{7,6},{8,7},{9,8},{10,9},{11,1... | collective-permute-start | bytes 393224 | tf_op jit(solution)/shard_map/ppermute | solution.py:13
  137.8 6.3 %collective-permute-start.7 = (bf16[2,256,128]{2,0,1:T(2,128)(2,1)S(1)}, bf16[2,256,128]{2,0,1:T(2,128)(2,1)S(1)}, u32[]{:S(2)}, u32[]{:S(2)}) collective-permute-start(bf16[2,256,128]{2,0,1:T(2,128)(2,1)S(1)} %copy.22), channel_id=1, source_target_pairs={{2,0},{3,1},{4,2},{5,3},{6,4},{7,5},{8,6},{9,7},{10,8},{11,9},{12,... | collective-permute-start | bytes 393224 | tf_op jit(solution)/shard_map/ppermute | solution.py:13
  150.3 6.0 %collective-permute-start.16 = (bf16[2,256,128]{2,0,1:T(2,128)(2,1)}, bf16[2,256,128]{2,0,1:T(2,128)(2,1)}, u32[]{:S(2)}, u32[]{:S(2)}) collective-permute-start(bf16[2,256,128]{2,0,1:T(2,128)(2,1)} %get-tuple-element.11), channel_id=1, source_target_pairs={{1,0},{2,1},{3,2},{4,3},{5,4},{6,5},{7,6},{8,7},{9,8},{10,9},{11,1... | collective-permute-start | bytes 393224 | tf_op jit(solution)/shard_map/ppermute | solution.py:13
  156.3 6.5 %concatenate.10 = bf16[16,256,128]{2,0,1:T(8,128)(2,1)} concatenate(bf16[8,256,128]{2,0,1:T(8,128)(2,1)} %copy-done.6, bf16[2,256,128]{2,0,1:T(2,128)(2,1)} %collective-permute-done.4, bf16[2,256,128]{2,0,1:T(2,128)(2,1)} %collective-permute-done.5, bf16[2,256,128]{2,0,1:T(2,128)(2,1)S(1)} %collective-permute-done.6, bf16[2,256,128]{2,0,1:T(2,128)(2,1)S(1)} %collective-permute-done.7), dimensions={0} | concatenate | bytes 2097152 | tf_op jit(solution)/shard_map/concatenate | solution.py:55
  165.3 3.3 gather_fusion.9
  168.6 3.8 fusion.20
  194.7 3.1 gather_fusion.17
  197.9 3.2 fusion.12
  209.1 5.4 %collective-permute-start.10 = (bf16[2,256,128]{2,0,1:T(2,128)(2,1)S(1)}, bf16[2,256,128]{2,0,1:T(2,128)(2,1)S(1)}, u32[]{:S(2)}, u32[]{:S(2)}) collective-permute-start(bf16[2,256,128]{2,0,1:T(2,128)(2,1)S(1)} %copy.31), channel_id=1, source_target_pairs={{0,2},{1,3},{2,4},{3,5},{4,6},{5,7},{6,8},{7,9},{8,10},{9,11},{10,... | collective-permute-start | bytes 393224 | tf_op jit(solution)/shard_map/ppermute | solution.py:13
  214.7 3.0 collective-permute-start.11
  220.7 5.2 collective-permute-start.9
  229.5 4.8 collective-permute-start.23
  234.3 3.4 collective-permute-start.20
  237.8 6.5 %concatenate.11 = bf16[16,256,128]{2,0,1:T(8,128)(2,1)} concatenate(bf16[8,256,128]{2,0,1:T(8,128)(2,1)} %copy-done.14, bf16[2,256,128]{2,0,1:T(2,128)(2,1)} %copy-done.31, bf16[2,256,128]{2,0,1:T(2,128)(2,1)} %collective-permute-done.9, bf16[2,256,128]{2,0,1:T(2,128)(2,1)} %copy-done.29, bf16[2,256,128]{2,0,1:T(2,128)(2,1)} %copy-done.30), dimensions={0} | concatenate | bytes 2097152 | tf_op jit(solution)/shard_map/concatenate | solution.py:55
  246.8 3.3 gather_fusion.14
  250.1 3.8 fusion.18
  267.3 46.2 %all-reduce.3.cloned.1.call-done = f32[4,128,128]{2,1,0:T(8,128)} async-done(((f32[4,128,128]{2,1,0:T(8,128)}), f32[4,128,128]{2,1,0:T(8,128)}) %all-reduce.3.cloned.1.call-update) | async-done | bytes 262160 | tf_op jit(solution)/shard_map/psum | solution.py:116
  313.5 3.4 fusion.60
  319.4 214.5 %all-reduce.5.cloned.1.call-done = f32[4,128,128]{2,1,0:T(8,128)} async-done(((f32[4,128,128]{2,1,0:T(8,128)}), f32[4,128,128]{2,1,0:T(8,128)}) %all-reduce.5.cloned.1.call-update) | async-done | bytes 262160 | tf_op jit(solution)/shard_map/psum | solution.py:117
  (208 shorter events, 135.9 us)
Async XLA Ops:
  7.2 306.3 %all-reduce.3.cloned.1.call-start = ((), (), s32[]{:S(2)}) async-start(), calls=%async_computation | async-start | bytes 524288 | tf_op jit(solution)/shard_map/psum | solution.py:116
  23.5 26.8 %copy-start.22 = (bf16[4,128,128]{2,1,0:T(8,128)(2,1)S(1)}, bf16[4,128,128]{2,1,0:T(8,128)(2,1)}, u32[]{:S(2)}) copy-start(bf16[4,128,128]{2,1,0:T(8,128)(2,1)} %param.10) | copy-start | bytes 393220
  24.7 75.7 %collective-permute-start.15 = (bf16[2,256,128]{2,0,1:T(2,128)(2,1)}, bf16[2,256,128]{2,0,1:T(2,128)(2,1)}, u32[]{:S(2)}, u32[]{:S(2)}) collective-permute-start(bf16[2,256,128]{2,0,1:T(2,128)(2,1)} %get-tuple-element.16), channel_id=1, source_target_pairs={{0,2},{1,3},{2,4},{3,5},{4,6},{5,7},{6,8},{7,9},{8,10},{9,11},{10,... | collective-permute-start | bytes 393224 | tf_op jit(solution)/shard_map/ppermute | solution.py:13
  29.8 72.1 %collective-permute-start.14 = (bf16[2,256,128]{2,0,1:T(2,128)(2,1)}, bf16[2,256,128]{2,0,1:T(2,128)(2,1)}, u32[]{:S(2)}, u32[]{:S(2)}) collective-permute-start(bf16[2,256,128]{2,0,1:T(2,128)(2,1)} %get-tuple-element.17), channel_id=1, source_target_pairs={{2,0},{3,1},{4,2},{5,3},{6,4},{7,5},{8,6},{9,7},{10,8},{11,9},{12,... | collective-permute-start | bytes 393224 | tf_op jit(solution)/shard_map/ppermute | solution.py:13
  32.9 70.3 %collective-permute-start.13 = (bf16[2,256,128]{2,0,1:T(2,128)(2,1)}, bf16[2,256,128]{2,0,1:T(2,128)(2,1)}, u32[]{:S(2)}, u32[]{:S(2)}) collective-permute-start(bf16[2,256,128]{2,0,1:T(2,128)(2,1)} %get-tuple-element.18), channel_id=1, source_target_pairs={{0,1},{1,2},{2,3},{3,4},{4,5},{5,6},{6,7},{7,8},{8,9},{9,10},{10,1... | collective-permute-start | bytes 393224 | tf_op jit(solution)/shard_map/ppermute | solution.py:13
  39.4 25.9 %collective-permute-start = (bf16[2,256,128]{2,1,0:T(8,128)(2,1)}, bf16[2,256,128]{2,1,0:T(8,128)(2,1)S(1)}, u32[]{:S(2)}, u32[]{:S(2)}) collective-permute-start(bf16[2,256,128]{2,1,0:T(8,128)(2,1)} %gather_fusion), channel_id=1, source_target_pairs={{0,1},{1,2},{2,3},{3,4},{4,5},{5,6},{6,7},{7,8},{8,9},{9,10},{10,1... | collective-permute-start | bytes 393224 | tf_op jit(solution)/shard_map/ppermute | solution.py:13
  44.8 23.0 %collective-permute-start.1 = (bf16[2,256,128]{2,1,0:T(8,128)(2,1)}, bf16[2,256,128]{2,1,0:T(8,128)(2,1)S(1)}, u32[]{:S(2)}, u32[]{:S(2)}) collective-permute-start(bf16[2,256,128]{2,1,0:T(8,128)(2,1)} %gather_fusion.1), channel_id=1, source_target_pairs={{1,0},{2,1},{3,2},{4,3},{5,4},{6,5},{7,6},{8,7},{9,8},{10,9},{11,1... | collective-permute-start | bytes 393224 | tf_op jit(solution)/shard_map/ppermute | solution.py:13
  65.3 9.6 %collective-permute-start.2 = (bf16[2,256,128]{2,1,0:T(8,128)(2,1)}, bf16[2,256,128]{2,1,0:T(8,128)(2,1)S(1)}, u32[]{:S(2)}, u32[]{:S(2)}) collective-permute-start(bf16[2,256,128]{2,1,0:T(8,128)(2,1)} %gather_fusion.2), channel_id=1, source_target_pairs={{0,2},{1,3},{2,4},{3,5},{4,6},{5,7},{6,8},{7,9},{8,10},{9,11},{10,... | collective-permute-start | bytes 393224 | tf_op jit(solution)/shard_map/ppermute | solution.py:13
  67.9 10.3 %collective-permute-start.3 = (bf16[2,256,128]{2,1,0:T(8,128)(2,1)}, bf16[2,256,128]{2,1,0:T(8,128)(2,1)S(1)}, u32[]{:S(2)}, u32[]{:S(2)}) collective-permute-start(bf16[2,256,128]{2,1,0:T(8,128)(2,1)} %gather_fusion.3), channel_id=1, source_target_pairs={{2,0},{3,1},{4,2},{5,3},{6,4},{7,5},{8,6},{9,7},{10,8},{11,9},{12,... | collective-permute-start | bytes 393224 | tf_op jit(solution)/shard_map/ppermute | solution.py:13
  74.9 29.6 %collective-permute-start.12 = (bf16[2,256,128]{2,0,1:T(2,128)(2,1)}, bf16[2,256,128]{2,0,1:T(2,128)(2,1)}, u32[]{:S(2)}, u32[]{:S(2)}) collective-permute-start(bf16[2,256,128]{2,0,1:T(2,128)(2,1)} %get-tuple-element.15), channel_id=1, source_target_pairs={{1,0},{2,1},{3,2},{4,3},{5,4},{6,5},{7,6},{8,7},{9,8},{10,9},{11,1... | collective-permute-start | bytes 393224 | tf_op jit(solution)/shard_map/ppermute | solution.py:13
  119.0 26.4 %copy-start.12 = (f32[16,256,128]{2,0,1:T(8,128)}, f32[16,256,128]{2,0,1:T(8,128)S(1)}, u32[]{:S(2)}) copy-start(f32[16,256,128]{2,0,1:T(8,128)S(1)} %fusion.2) | copy-start | bytes 6291460
  119.0 25.1 %copy-start.8 = (bf16[8,256,128]{2,1,0:T(8,128)(2,1)S(1)}, bf16[8,256,128]{2,1,0:T(8,128)(2,1)}, u32[]{:S(2)}) copy-start(bf16[8,256,128]{2,1,0:T(8,128)(2,1)} %copy.14) | copy-start | bytes 1572868
  119.0 25.1 %copy-start.18 = (f32[2048,128]{1,0:T(8,128)S(1)}, f32[2048,128]{1,0:T(8,128)}, u32[]{:S(2)}) copy-start(f32[2048,128]{1,0:T(8,128)} %fusion.70) | copy-start | bytes 3145732
  120.1 67.1 %collective-permute-start.19 = (bf16[2,256,128]{2,0,1:T(2,128)(2,1)}, bf16[2,256,128]{2,0,1:T(2,128)(2,1)}, u32[]{:S(2)}, u32[]{:S(2)}) collective-permute-start(bf16[2,256,128]{2,0,1:T(2,128)(2,1)} %get-tuple-element.12), channel_id=1, source_target_pairs={{0,2},{1,3},{2,4},{3,5},{4,6},{5,7},{6,8},{7,9},{8,10},{9,11},{10,... | collective-permute-start | bytes 393224 | tf_op jit(solution)/shard_map/ppermute | solution.py:13
  127.1 19.3 %collective-permute-start.4 = (bf16[2,256,128]{2,0,1:T(2,128)(2,1)S(1)}, bf16[2,256,128]{2,0,1:T(2,128)(2,1)}, u32[]{:S(2)}, u32[]{:S(2)}) collective-permute-start(bf16[2,256,128]{2,0,1:T(2,128)(2,1)S(1)} %copy.16), channel_id=1, source_target_pairs={{0,1},{1,2},{2,3},{3,4},{4,5},{5,6},{6,7},{7,8},{8,9},{9,10},{10,1... | collective-permute-start | bytes 393224 | tf_op jit(solution)/shard_map/ppermute | solution.py:13
  129.2 19.1 %collective-permute-start.5 = (bf16[2,256,128]{2,0,1:T(2,128)(2,1)S(1)}, bf16[2,256,128]{2,0,1:T(2,128)(2,1)}, u32[]{:S(2)}, u32[]{:S(2)}) collective-permute-start(bf16[2,256,128]{2,0,1:T(2,128)(2,1)S(1)} %copy.18), channel_id=1, source_target_pairs={{1,0},{2,1},{3,2},{4,3},{5,4},{6,5},{7,6},{8,7},{9,8},{10,9},{11,1... | collective-permute-start | bytes 393224 | tf_op jit(solution)/shard_map/ppermute | solution.py:13
  135.7 14.5 %collective-permute-start.6 = (bf16[2,256,128]{2,0,1:T(2,128)(2,1)S(1)}, bf16[2,256,128]{2,0,1:T(2,128)(2,1)S(1)}, u32[]{:S(2)}, u32[]{:S(2)}) collective-permute-start(bf16[2,256,128]{2,0,1:T(2,128)(2,1)S(1)} %copy.20), channel_id=1, source_target_pairs={{0,2},{1,3},{2,4},{3,5},{4,6},{5,7},{6,8},{7,9},{8,10},{9,11},{10,... | collective-permute-start | bytes 393224 | tf_op jit(solution)/shard_map/ppermute | solution.py:13
  137.8 18.5 %collective-permute-start.7 = (bf16[2,256,128]{2,0,1:T(2,128)(2,1)S(1)}, bf16[2,256,128]{2,0,1:T(2,128)(2,1)S(1)}, u32[]{:S(2)}, u32[]{:S(2)}) collective-permute-start(bf16[2,256,128]{2,0,1:T(2,128)(2,1)S(1)} %copy.22), channel_id=1, source_target_pairs={{2,0},{3,1},{4,2},{5,3},{6,4},{7,5},{8,6},{9,7},{10,8},{11,9},{12,... | collective-permute-start | bytes 393224 | tf_op jit(solution)/shard_map/ppermute | solution.py:13
  146.4 42.3 %collective-permute-start.18 = (bf16[2,256,128]{2,0,1:T(2,128)(2,1)}, bf16[2,256,128]{2,0,1:T(2,128)(2,1)}, u32[]{:S(2)}, u32[]{:S(2)}) collective-permute-start(bf16[2,256,128]{2,0,1:T(2,128)(2,1)} %get-tuple-element.13), channel_id=1, source_target_pairs={{2,0},{3,1},{4,2},{5,3},{6,4},{7,5},{8,6},{9,7},{10,8},{11,9},{12,... | collective-permute-start | bytes 393224 | tf_op jit(solution)/shard_map/ppermute | solution.py:13
  148.3 41.7 %collective-permute-start.17 = (bf16[2,256,128]{2,0,1:T(2,128)(2,1)}, bf16[2,256,128]{2,0,1:T(2,128)(2,1)}, u32[]{:S(2)}, u32[]{:S(2)}) collective-permute-start(bf16[2,256,128]{2,0,1:T(2,128)(2,1)} %get-tuple-element.14), channel_id=1, source_target_pairs={{0,1},{1,2},{2,3},{3,4},{4,5},{5,6},{6,7},{7,8},{8,9},{9,10},{10,1... | collective-permute-start | bytes 393224 | tf_op jit(solution)/shard_map/ppermute | solution.py:13
  150.3 41.1 %collective-permute-start.16 = (bf16[2,256,128]{2,0,1:T(2,128)(2,1)}, bf16[2,256,128]{2,0,1:T(2,128)(2,1)}, u32[]{:S(2)}, u32[]{:S(2)}) collective-permute-start(bf16[2,256,128]{2,0,1:T(2,128)(2,1)} %get-tuple-element.11), channel_id=1, source_target_pairs={{1,0},{2,1},{3,2},{4,3},{5,4},{6,5},{7,6},{8,7},{9,8},{10,9},{11,1... | collective-permute-start | bytes 393224 | tf_op jit(solution)/shard_map/ppermute | solution.py:13
  205.7 21.4 %copy-start.9 = (f32[16,256,128]{2,0,1:T(8,128)}, f32[16,256,128]{2,0,1:T(8,128)S(1)}, u32[]{:S(2)}) copy-start(f32[16,256,128]{2,0,1:T(8,128)S(1)} %fusion) | copy-start | bytes 6291460
  205.7 20.1 %copy-start.7 = (bf16[8,256,128]{2,1,0:T(8,128)(2,1)S(1)}, bf16[8,256,128]{2,1,0:T(8,128)(2,1)}, u32[]{:S(2)}) copy-start(bf16[8,256,128]{2,1,0:T(8,128)(2,1)} %copy.25) | copy-start | bytes 1572868
  206.9 53.5 %collective-permute-start.22 = (bf16[2,256,128]{2,0,1:T(2,128)(2,1)}, bf16[2,256,128]{2,0,1:T(2,128)(2,1)}, u32[]{:S(2)}, u32[]{:S(2)}) collective-permute-start(bf16[2,256,128]{2,0,1:T(2,128)(2,1)} %get-tuple-element.9), channel_id=1, source_target_pairs={{2,0},{3,1},{4,2},{5,3},{6,4},{7,5},{8,6},{9,7},{10,8},{11,9},{12,... | collective-permute-start | bytes 393224 | tf_op jit(solution)/shard_map/ppermute | solution.py:13
  209.1 18.5 %collective-permute-start.10 = (bf16[2,256,128]{2,0,1:T(2,128)(2,1)S(1)}, bf16[2,256,128]{2,0,1:T(2,128)(2,1)S(1)}, u32[]{:S(2)}, u32[]{:S(2)}) collective-permute-start(bf16[2,256,128]{2,0,1:T(2,128)(2,1)S(1)} %copy.31), channel_id=1, source_target_pairs={{0,2},{1,3},{2,4},{3,5},{4,6},{5,7},{6,8},{7,9},{8,10},{9,11},{10,... | collective-permute-start | bytes 393224 | tf_op jit(solution)/shard_map/ppermute | solution.py:13
  214.7 14.8 %collective-permute-start.11 = (bf16[2,256,128]{2,0,1:T(2,128)(2,1)S(1)}, bf16[2,256,128]{2,0,1:T(2,128)(2,1)S(1)}, u32[]{:S(2)}, u32[]{:S(2)}) collective-permute-start(bf16[2,256,128]{2,0,1:T(2,128)(2,1)S(1)} %copy.33), channel_id=1, source_target_pairs={{2,0},{3,1},{4,2},{5,3},{6,4},{7,5},{8,6},{9,7},{10,8},{11,9},{12,... | collective-permute-start | bytes 393224 | tf_op jit(solution)/shard_map/ppermute | solution.py:13
  217.8 16.5 %collective-permute-start.8 = (bf16[2,256,128]{2,0,1:T(2,128)(2,1)S(1)}, bf16[2,256,128]{2,0,1:T(2,128)(2,1)S(1)}, u32[]{:S(2)}, u32[]{:S(2)}) collective-permute-start(bf16[2,256,128]{2,0,1:T(2,128)(2,1)S(1)} %copy.27), channel_id=1, source_target_pairs={{0,1},{1,2},{2,3},{3,4},{4,5},{5,6},{6,7},{7,8},{8,9},{9,10},{10,1... | collective-permute-start | bytes 393224 | tf_op jit(solution)/shard_map/ppermute | solution.py:13
  220.7 17.1 %collective-permute-start.9 = (bf16[2,256,128]{2,0,1:T(2,128)(2,1)S(1)}, bf16[2,256,128]{2,0,1:T(2,128)(2,1)}, u32[]{:S(2)}, u32[]{:S(2)}) collective-permute-start(bf16[2,256,128]{2,0,1:T(2,128)(2,1)S(1)} %copy.29), channel_id=1, source_target_pairs={{1,0},{2,1},{3,2},{4,3},{5,4},{6,5},{7,6},{8,7},{9,8},{10,9},{11,1... | collective-permute-start | bytes 393224 | tf_op jit(solution)/shard_map/ppermute | solution.py:13
  227.6 35.1 %collective-permute-start.21 = (bf16[2,256,128]{2,0,1:T(2,128)(2,1)}, bf16[2,256,128]{2,0,1:T(2,128)(2,1)}, u32[]{:S(2)}, u32[]{:S(2)}) collective-permute-start(bf16[2,256,128]{2,0,1:T(2,128)(2,1)} %get-tuple-element.10), channel_id=1, source_target_pairs={{0,1},{1,2},{2,3},{3,4},{4,5},{5,6},{6,7},{7,8},{8,9},{9,10},{10,1... | collective-permute-start | bytes 393224 | tf_op jit(solution)/shard_map/ppermute | solution.py:13
  229.5 35.4 %collective-permute-start.23 = (bf16[2,256,128]{2,0,1:T(2,128)(2,1)}, bf16[2,256,128]{2,0,1:T(2,128)(2,1)}, u32[]{:S(2)}, u32[]{:S(2)}) collective-permute-start(bf16[2,256,128]{2,0,1:T(2,128)(2,1)} %get-tuple-element.8), channel_id=1, source_target_pairs={{0,2},{1,3},{2,4},{3,5},{4,6},{5,7},{6,8},{7,9},{8,10},{9,11},{10,... | collective-permute-start | bytes 393224 | tf_op jit(solution)/shard_map/ppermute | solution.py:13
  234.3 79.2 %collective-permute-start.20 = (bf16[2,256,128]{2,0,1:T(2,128)(2,1)}, bf16[2,256,128]{2,0,1:T(2,128)(2,1)S(1)}, u32[]{:S(2)}, u32[]{:S(2)}) collective-permute-start(bf16[2,256,128]{2,0,1:T(2,128)(2,1)} %get-tuple-element.7), channel_id=1, source_target_pairs={{1,0},{2,1},{3,2},{4,3},{5,4},{6,5},{7,6},{8,7},{9,8},{10,9},{11,1... | collective-permute-start | bytes 393224 | tf_op jit(solution)/shard_map/ppermute | solution.py:13
  260.3 273.6 %all-reduce.5.cloned.1.call-start = ((), (), s32[]{:S(2)}) async-start(), calls=%async_computation.1 | async-start | bytes 524288 | tf_op jit(solution)/shard_map/psum | solution.py:117
  (37 other events, 193.9 us)
Sparse Core Ops, SparseCore 0:
  260.4 52.9 all-reduce.2
  319.7 214.0 all-reduce.4
